TPU v7x, 32 devices: a whole 2x2x4 slice. The times are simulated.
32 devices in a mesh: grp: 2 (over x), bus: 16 (over z, y, core).
Axes of the slice: x: 2, y: 2, z: 4, core: 2. Of those that a mesh axis runs over, the one named last changes fastest.
Arguments:
- series: bfloat16 [32, 2048, 1024], P(('grp', 'bus')), parts along dimension 0, may hold values from -6 to 6
- hour_ids: int32 [32], P(('grp', 'bus')), parts along dimension 0, may hold values from 0 to 23
- hour_table: bfloat16 [24, 1024], replicated, may hold values from -3 to 3
- norm_gain: float32 [1024], replicated, may hold values from 0.1 to 1.9
- bus_order: int32 [4096], P('grp'), parts along dimension 0, may hold values from 0 to 2047, each once
- w_query: bfloat16 [1024, 512], replicated, may hold values from -0.1875 to 0.1875
- w_key: bfloat16 [1024, 512], replicated, may hold values from -0.1875 to 0.1875
- w_value: bfloat16 [1024, 512], replicated, may hold values from -0.1875 to 0.1875
- score_scale: float32 [8], replicated, may hold values from 0.5 to 10, as said below
- neighbors: int32 [32, 3], P('grp'), parts along dimension 0, may hold values from -1 to 15, as said below
- grad_out: bfloat16 [32, 2048, 512], P('grp', 'bus'), parts along dimension 0, may hold values from -6 to 6
Outputs:
- key_grad: bfloat16 [32, 2048, 512], P('grp', 'bus'), parts along dimension 0
- value_grad: bfloat16 [32, 2048, 512], P('grp', 'bus'), parts along dimension 0
There are 2 independent parts, one for each index of `grp`. A program takes and returns all parts, laid end to end along the dimension named above; an argument that names none is the same for every part. Nothing has to cross between parts.
Inputs may be any that keep to these rules, and one draw needn't show every extreme that they name: `neighbors`: row b lists the key blocks read by query block b: entry 0 is b - 1 or -1, entry 1 is b, entry 2 is b + 1 or -1; -1 marks a block not read, and stands in entry 0 of row 0 and entry 2 of row 15. `score_scale`: positive temperatures of the heads.
All inputs are finite; a program needn't handle non-finite values.
Results may differ from a plain program's by a relative error of at most 0.018.
The roundings to bfloat16 on the way count: a program that leaves them out, or rounds other values in their place, can miss the bound.
Values may be sent and summed in bfloat16 or wider, within the bound.
No kernel may reach another device: no remote copies, remote signals or barrier semaphores. Data moves between devices by JAX's collectives and lax.ppermute only.
A program may use at most 256 MiB of HBM per device.

v0:
```python
import math
import jax
import jax.numpy as jnp
from jax import lax
from jax.sharding import PartitionSpec as P

EPSILON = 1e-05
NEG_FILL = -1e30


def with_halo(shard, sides, width):
    for axis, dim in sides:
        devices, length = (lax.axis_size(axis), shard.shape[dim])
        up = [(i, (i + 1) % devices) for i in range(devices - 1)]
        down = [(j, i) for i, j in up]
        last = lax.slice_in_dim(shard, length - width, length, axis=dim)
        leading = lax.slice_in_dim(shard, 0, width, axis=dim)
        before = lax.ppermute(last, axis, up)
        after = lax.ppermute(leading, axis, down)
        shard = jnp.concatenate([before, shard, after], axis=dim)
    return shard


def from_behind(value, axis, steps):
    count = lax.axis_size(axis)
    leading, last = (max(0, -steps), min(count, count - steps))
    return lax.ppermute(value, axis, [(source, source + steps) for source in range(leading, last)])


def split_heads(array, head_count):
    return array.reshape(array.shape[0], array.shape[1], head_count, array.shape[2] // head_count)


def over_groups(step_fn, arrays, group_size):
    stacked = tuple(
        (
            item.reshape((item.shape[0] // group_size, group_size) + item.shape[1:])
            for item in arrays
        )
    )
    results = lax.map(lambda pieces: step_fn(*pieces), stacked)
    return tuple((item.reshape((-1,) + item.shape[2:]) for item in results))


def reader_terms(queries, key_tiles, value_tiles, grad_rows, colvalid, head_scale):
    scores = (
        jnp.einsum("sihd,sjhd->shij", queries, key_tiles, preferred_element_type=jnp.float32)
        * head_scale[None, :, None, None]
    )
    scores = jnp.where(colvalid[None, None, None, :], scores, NEG_FILL)
    row_max = jnp.max(scores, axis=-1)
    log_total = row_max + jnp.log(jnp.sum(jnp.exp(scores - row_max[..., None]), axis=-1))
    weights = jnp.exp(scores - log_total[..., None])
    weights_b = weights.astype(jnp.bfloat16)
    attended = jnp.einsum(
        "shij,sjhd->sihd", weights_b, value_tiles, preferred_element_type=jnp.float32
    ).astype(jnp.bfloat16)
    row_dot = jnp.einsum("sihd,sihd->shi", grad_rows, attended, preferred_element_type=jnp.float32)
    dweights = jnp.einsum(
        "sihd,sjhd->shij", grad_rows, value_tiles, preferred_element_type=jnp.float32
    )
    dscores = (weights * (dweights - row_dot[..., None]) * head_scale[None, :, None, None]).astype(
        jnp.bfloat16
    )
    value_part = jnp.einsum(
        "shij,sihd->sjhd", weights_b, grad_rows, preferred_element_type=jnp.float32
    )
    key_part = jnp.einsum("shij,sihd->sjhd", dscores, queries, preferred_element_type=jnp.float32)
    return (log_total, row_dot, key_part.astype(jnp.bfloat16), value_part.astype(jnp.bfloat16))


def on_device(
    series,
    hour_ids,
    hour_table,
    norm_gain,
    bus_order,
    w_query,
    w_key,
    w_value,
    score_scale,
    neighbors,
    grad_out,
):
    head_count = score_scale.shape[0]
    snap_count = grad_out.shape[0]
    block_rows = grad_out.shape[1]
    feat_width = grad_out.shape[2]
    head_dim = feat_width // head_count
    ordered = jnp.take(series, bus_order, axis=1)
    onehot = (
        hour_ids[:, None] == jnp.arange(hour_table.shape[0], dtype=jnp.int32)[None, :]
    ).astype(jnp.bfloat16)
    hour_rows = jnp.dot(onehot, hour_table, preferred_element_type=jnp.float32)
    mixed = ordered.astype(jnp.float32) + hour_rows[:, None, :]
    normed = (
        mixed * lax.rsqrt(jnp.mean(mixed * mixed, axis=-1, keepdims=True) + EPSILON) * norm_gain
    ).astype(jnp.bfloat16)
    arrived = lax.all_to_all(normed, "bus", split_axis=1, concat_axis=0, tiled=True)
    flat_rows = arrived.reshape(-1, arrived.shape[2])
    queries, key_rows, value_rows = [
        jnp.dot(flat_rows, weight, preferred_element_type=jnp.float32)
        .astype(jnp.bfloat16)
        .reshape(snap_count, block_rows, feat_width)
        for weight in (w_query, w_key, w_value)
    ]
    dev_index = lax.axis_index("bus")
    own_row = lax.dynamic_slice_in_dim(neighbors, dev_index, 1, 0)[0]
    colvalid = jnp.repeat(own_row >= 0, block_rows)
    head_scale = score_scale / math.sqrt(head_dim)
    group_size = math.gcd(snap_count, max(1, 512 // block_rows))
    kv_tiles = with_halo(jnp.stack([key_rows, value_rows]), (("bus", 2),), block_rows)
    query_heads = split_heads(queries, head_count)
    grad_heads = split_heads(grad_out, head_count)
    key_heads = split_heads(kv_tiles[0], head_count)
    value_heads = split_heads(kv_tiles[1], head_count)

    def full_step(query_part, key_part, value_part, grad_part):
        return reader_terms(query_part, key_part, value_part, grad_part, colvalid, head_scale)

    log_total, row_dot, key_part, value_part = over_groups(
        full_step, (query_heads, key_heads, value_heads, grad_heads), group_size
    )
    partials = jnp.stack(
        [
            key_part.reshape(snap_count, 3 * block_rows, feat_width),
            value_part.reshape(snap_count, 3 * block_rows, feat_width),
        ]
    )
    from_upper = from_behind(partials[:, :, :block_rows], "bus", -1)
    from_lower = from_behind(partials[:, :, 2 * block_rows :], "bus", 1)
    summed = (
        partials[:, :, block_rows : 2 * block_rows].astype(jnp.float32)
        + from_lower.astype(jnp.float32)
        + from_upper.astype(jnp.float32)
    )
    key_grad = summed[0].astype(jnp.bfloat16)
    value_grad = summed[1].astype(jnp.bfloat16)
    return (key_grad, value_grad)


def solution(mesh):
    return jax.shard_map(
        on_device,
        mesh=mesh,
        in_specs=(
            P(("grp", "bus"), None, None),
            P(("grp", "bus")),
            P(),
            P(),
            P("grp"),
            P(),
            P(),
            P(),
            P(),
            P("grp", None),
            P("grp", "bus", None),
        ),
        out_specs=(P("grp", "bus", None), P("grp", "bus", None)),
        check_vma=False,
    )
```

profile of v0, /device:TPU:12, one launch (start us, length us, event | category | flops | bytes accessed | tf_op | source)
XLA Modules:
  0.0 511.9 jit_solution(18104541909109588138)
XLA Ops:
  0.6 0.0 copy-start
  0.6 0.8 fusion.71
  1.4 0.7 compare_and_fusion
  2.8 0.0 copy-start.8
  2.8 0.0 copy-start.9
  2.8 13.7 %gather_fusion = bf16[2048,1024]{1,0:T(8,128)(2,1)} fusion(bf16[2048,1024]{1,0:T(8,128)(2,1)} %bitcast.128, s32[2048]{0:T(1024)S(1)} %fusion.71), kind=kCustom, calls=%fused_computation | custom fusion | bytes 8396800 | tf_op jit(solution)/shard_map/jit(_take)/gather | solution.py:90
  16.5 0.1 fusion.73
  16.6 3.6 multiply_reduce_fusion
  20.3 1.7 multiply_convert_fusion.6
  22.0 28.7 %copy.65 = bf16[1,2048,1024]{2,0,1:T(2,128)(2,1)} copy(bf16[1,2048,1024]{2,1,0:T(8,128)(2,1)S(1)} %multiply_convert_fusion.6) | data formatting | bytes 8388608 | tf_op jit(solution)/shard_map/convert_element_type | solution.py:98
  50.7 0.5 broadcast.169
  51.3 25.9 %reduce.5 = bf16[2048,1024]{1,0:T(8,128)(2,1)} reduce(bf16[2048,1,1024]{2,1,0:T(2,128)(2,1)} %bitcast.129, bf16[]{:T(256)} %broadcast.169), dimensions={1}, to_apply=%bitcast.102.reduce_sub_computation | reduce | bytes 8388610
  77.2 11.4 %reshape.223 = bf16[16,2,65536]{2,1,0:T(2,128)(2,1)} reshape(bf16[2048,1024]{1,0:T(8,128)(2,1)} %reduce.5) | data formatting | bytes 8388608
  88.6 98.4 %all_to_all.4 = bf16[16,2,65536]{2,1,0:T(2,128)(2,1)} all-to-all(bf16[16,2,65536]{2,1,0:T(2,128)(2,1)} %reshape.223), channel_id=1, replica_groups=mesh['grp'=2,'bus'=16] {'bus'}, dimensions={0} | all-to-all | bytes 8388608 | tf_op jit(solution)/shard_map/all_to_all | solution.py:99
  187.0 12.3 %reshape.224 = bf16[2048,1,1024]{2,1,0:T(2,128)(2,1)} reshape(bf16[16,2,65536]{2,1,0:T(2,128)(2,1)} %all_to_all.4) | data formatting | bytes 8388608
  199.3 7.1 %fusion.65 = bf16[2048,512]{1,0:T(8,128)(2,1)} fusion(bf16[1024,512]{1,0:T(8,128)(2,1)S(1)} %copy-done, bf16[1,2048,1024]{2,0,1:T(2,128)(2,1)} %bitcast.135), kind=kOutput, calls=%fused_computation.64 | convolution fusion | flops 2148532224 | bytes 7340032 | tf_op jit(solution)/shard_map/dot_general | solution.py:102
  206.4 3.0 copy.36
  209.5 7.3 %fusion.68 = bf16[2048,512]{1,0:T(8,128)(2,1)} fusion(bf16[1024,512]{1,0:T(8,128)(2,1)} %param.20, bf16[1,2048,1024]{2,0,1:T(2,128)(2,1)} %bitcast.136), kind=kOutput, calls=%fused_computation.65 | convolution fusion | flops 2148532224 | bytes 7340032 | tf_op jit(solution)/shard_map/dot_general | solution.py:102
  216.8 3.9 copy.37
  220.7 3.9 pad_maximum_fusion.2
  224.7 2.2 collective-permute-start
  226.9 3.6 collective-permute-start.1
  230.5 3.9 copy.38
  234.4 0.2 fusion.72
  234.6 7.3 %fusion.62 = bf16[2048,512]{1,0:T(8,128)(2,1)} fusion(bf16[1024,512]{1,0:T(8,128)(2,1)} %param.18, bf16[1,2048,1024]{2,0,1:T(2,128)(2,1)} %bitcast.137), kind=kOutput, calls=%fused_computation.63 | convolution fusion | flops 2148532224 | bytes 7340032 | tf_op jit(solution)/shard_map/dot_general | solution.py:102
  241.9 6.1 %reshape.221 = bf16[4,4,128,8,64]{4,3,2,1,0:T(8,128)(2,1)} reshape(bf16[2048,512]{1,0:T(8,128)(2,1)} %fusion.62) | data formatting | bytes 4194304 | tf_op jit(solution)/shard_map/reshape;reshape;reshape | solution.py:37
  248.1 5.1 copy.39
  253.1 66.6 %collective-permute-done = bf16[2,16,128,512]{2,3,1,0:T(8,128)(2,1)} collective-permute-done((bf16[2,16,128,512]{2,3,1,0:T(8,128)(2,1)}, bf16[2,16,128,512]{2,3,1,0:T(8,128)(2,1)}, u32[]{:S(2)}, u32[]{:S(2)}) %collective-permute-start) | collective-permute-done | bytes 4194336 | tf_op jit(solution)/shard_map/ppermute | solution.py:18
  319.7 6.3 %pad_maximum_fusion = bf16[2,16,384,512]{2,3,1,0:T(8,128)(2,1)S(1)} fusion(bf16[2,16,128,512]{2,3,1,0:T(8,128)(2,1)} %collective-permute-done.1, bf16[1,16,128,512]{2,3,1,0:T(8,128)(2,1)} %copy.37, bf16[1,16,128,512]{2,3,1,0:T(8,128)(2,1)S(1)} %copy.36, bf16[2,16,128,512]{2,3,1,0:T(8,128)(2,1)} %collective-permute-done), kind=kLoop, calls=%fused_computation.47 | loop fusion | flops 50331648 | bytes 25165824 | tf_op jit(solution)/shard_map/concatenate | solution.py:20
  326.1 5.9 %fusion.81 = (bf16[1,16,384,512]{2,3,1,0:T(8,128)(2,1)}, bf16[1,16,384,512]{2,3,1,0:T(8,128)(2,1)}) fusion(bf16[2,16,384,512]{2,3,1,0:T(8,128)(2,1)S(1)} %pad_maximum_fusion), kind=kLoop, calls=%fused_computation.83 | loop fusion | bytes 25165824 | tf_op jit(solution)/shard_map/slice | solution.py:116
  332.0 70.7 %while.13 = (s32[]{:T(128)}, bf16[4,4,384,8,64]{2,4,3,1,0:T(8,128)(2,1)}, bf16[4,4,384,8,64]{2,4,3,1,0:T(8,128)(2,1)}, bf16[4,4,128,8,64]{2,4,3,1,0:T(8,128)(2,1...) while((s32[]{:T(128)}, ...), condition=%wide.region_4.5_spmd.clone, body=%wide.region_1.0_spmd.clone.sunk | while | flops 1044111360 | bytes 75687264 | solution.py:41
  332.0 0.1 broadcast_bitcast_fusion.2
  332.1 2.8 fusion.102
  334.9 2.3 exponential_reduce_fusion.2
  337.2 2.8 bitcast_dynamic-update-slice_fusion.5
  340.1 3.4 fusion.103
  343.5 6.2 %bitcast_dynamic-update-slice_fusion.4 = bf16[4,4,384,8,64]{2,4,3,1,0:T(8,128)(2,1)} fusion(bf16[4,4,384,8,64]{2,4,3,1,0:T(8,128)(2,1)} %get-tuple-element.211, s32[]{:T(128)} %get-tuple-element.210, f32[4,8,128,384]{3,2,1,0:T(8,128)} %copy-done.2, f32[4,8,128]{2,1,0:T(8,128)S(1)} %fusion.103, f32[4,8,128]{2,1,0:T(8,128)S(1)} %log_add_fusion.2, ...), kind=kOutput, calls=%fused_computation.14.clone.1 | convolution fusion | flops 414449664 | bytes 10521600 | tf_op jit(solution)/shard_map/while/body/eval_jaxpr/shij,sihd->sjhd/dot_general | solution.py:68
  349.7 0.1 broadcast_bitcast_fusion.2
  349.7 2.8 fusion.102
  352.5 2.3 exponential_reduce_fusion.2
  354.9 2.8 bitcast_dynamic-update-slice_fusion.5
  357.7 3.4 fusion.103
  361.2 6.2 %bitcast_dynamic-update-slice_fusion.4 = bf16[4,4,384,8,64]{2,4,3,1,0:T(8,128)(2,1)} fusion(bf16[4,4,384,8,64]{2,4,3,1,0:T(8,128)(2,1)} %get-tuple-element.211, s32[]{:T(128)} %get-tuple-element.210, f32[4,8,128,384]{3,2,1,0:T(8,128)} %copy-done.2, f32[4,8,128]{2,1,0:T(8,128)S(1)} %fusion.103, f32[4,8,128]{2,1,0:T(8,128)S(1)} %log_add_fusion.2, ...), kind=kOutput, calls=%fused_computation.14.clone.1 | convolution fusion | flops 414449664 | bytes 10521600 | tf_op jit(solution)/shard_map/while/body/eval_jaxpr/shij,sihd->sjhd/dot_general | solution.py:68
  367.4 0.1 broadcast_bitcast_fusion.2
  367.4 2.8 fusion.102
  370.2 2.3 exponential_reduce_fusion.2
  372.6 2.9 bitcast_dynamic-update-slice_fusion.5
  375.5 3.4 fusion.103
  378.9 6.2 %bitcast_dynamic-update-slice_fusion.4 = bf16[4,4,384,8,64]{2,4,3,1,0:T(8,128)(2,1)} fusion(bf16[4,4,384,8,64]{2,4,3,1,0:T(8,128)(2,1)} %get-tuple-element.211, s32[]{:T(128)} %get-tuple-element.210, f32[4,8,128,384]{3,2,1,0:T(8,128)} %copy-done.2, f32[4,8,128]{2,1,0:T(8,128)S(1)} %fusion.103, f32[4,8,128]{2,1,0:T(8,128)S(1)} %log_add_fusion.2, ...), kind=kOutput, calls=%fused_computation.14.clone.1 | convolution fusion | flops 414449664 | bytes 10521600 | tf_op jit(solution)/shard_map/while/body/eval_jaxpr/shij,sihd->sjhd/dot_general | solution.py:68
  385.1 0.1 broadcast_bitcast_fusion.2
  385.1 2.8 fusion.102
  387.9 2.3 exponential_reduce_fusion.2
  390.3 2.8 bitcast_dynamic-update-slice_fusion.5
  393.1 3.4 fusion.103
  396.6 6.2 %bitcast_dynamic-update-slice_fusion.4 = bf16[4,4,384,8,64]{2,4,3,1,0:T(8,128)(2,1)} fusion(bf16[4,4,384,8,64]{2,4,3,1,0:T(8,128)(2,1)} %get-tuple-element.211, s32[]{:T(128)} %get-tuple-element.210, f32[4,8,128,384]{3,2,1,0:T(8,128)} %copy-done.2, f32[4,8,128]{2,1,0:T(8,128)S(1)} %fusion.103, f32[4,8,128]{2,1,0:T(8,128)S(1)} %log_add_fusion.2, ...), kind=kOutput, calls=%fused_computation.14.clone.1 | convolution fusion | flops 414449664 | bytes 10521600 | tf_op jit(solution)/shard_map/while/body/eval_jaxpr/shij,sihd->sjhd/dot_general | solution.py:68
  402.7 4.0 fusion.54
  406.7 2.6 collective-permute-start.2
  409.3 3.5 collective-permute-start.3
  412.8 88.9 %collective-permute-done.2 = bf16[2,16,128,512]{2,3,1,0:T(8,128)(2,1)S(1)} collective-permute-done((bf16[2,16,128,512]{2,3,1,0:T(8,128)(2,1)S(1)}, bf16[2,16,128,512]{2,3,1,0:T(8,128)(2,1)S(1)}, u32[]{:S(2)}, u32[]{:S(2)}) %collective-permute-start.2) | collective-permute-done | bytes 4194336 | tf_op jit(solution)/shard_map/ppermute | solution.py:27
  501.8 1.9 add_convert_fusion
  503.7 0.0 copy-start.1
  503.7 1.7 slice_bitcast_fusion
  505.4 3.9 copy.40
  509.3 2.6 copy.41
  (42 shorter events, 0.1 us)
Async XLA Ops:
  0.6 198.7 %copy-start = (bf16[1024,512]{1,0:T(8,128)(2,1)S(1)}, bf16[1024,512]{1,0:T(8,128)(2,1)}, u32[]{:S(2)}) copy-start(bf16[1024,512]{1,0:T(8,128)(2,1)} %param.19) | copy-start | bytes 3145732
  2.8 13.7 %copy-start.8 = (bf16[24,1024]{1,0:T(8,128)(2,1)S(1)}, bf16[24,1024]{1,0:T(8,128)(2,1)}, u32[]{:S(2)}) copy-start(bf16[24,1024]{1,0:T(8,128)(2,1)} %param.15) | copy-start | bytes 147460
  2.8 17.5 %copy-start.9 = (f32[1024]{0:T(1024)S(1)}, f32[1024]{0:T(1024)}, u32[]{:S(2)}) copy-start(f32[1024]{0:T(1024)} %param.16) | copy-start | bytes 12292
  16.5 3.8 copy-start.3
  220.7 13.7 %copy-start.10 = (s32[16,3]{0,1:T(4,128)S(1)}, s32[16,3]{0,1:T(4,128)}, u32[]{:S(2)}) copy-start(s32[16,3]{0,1:T(4,128)} %param.22) | copy-start | bytes 580
  220.7 13.9 %copy-start.11 = (f32[8]{0:T(128)S(1)}, f32[8]{0:T(128)}, u32[]{:S(2)}) copy-start(f32[8]{0:T(128)} %param.21) | copy-start | bytes 100
  224.7 95.1 %collective-permute-start = (bf16[2,16,128,512]{2,3,1,0:T(8,128)(2,1)}, bf16[2,16,128,512]{2,3,1,0:T(8,128)(2,1)}, u32[]{:S(2)}, u32[]{:S(2)}) collective-permute-start(bf16[2,16,128,512]{2,3,1,0:T(8,128)(2,1)} %pad_maximum_fusion.2), channel_id=1, source_target_pairs={{0,1},{1,2},{2,3},{3,4},{4,5},{5,6},{6,7},{7,8},{8,9},{9,10},{10,1... | collective-permute-start | bytes 12582920 | tf_op jit(solution)/shard_map/ppermute | solution.py:18
  226.9 92.9 %collective-permute-start.1 = (bf16[2,16,128,512]{2,3,1,0:T(8,128)(2,1)}, bf16[2,16,128,512]{2,3,1,0:T(8,128)(2,1)}, u32[]{:S(2)}, u32[]{:S(2)}) collective-permute-start(bf16[2,16,128,512]{2,3,1,0:T(8,128)(2,1)} %pad_maximum_fusion.2), channel_id=1, source_target_pairs={{1,0},{2,1},{3,2},{4,3},{5,4},{6,5},{7,6},{8,7},{9,8},{10,9},{11,1... | collective-permute-start | bytes 12582920 | tf_op jit(solution)/shard_map/ppermute | solution.py:19
  326.1 6.0 %copy-start.6 = (bf16[4,4,128,8,64]{2,4,3,1,0:T(8,128)(2,1)S(1)}, bf16[4,4,128,8,64]{2,4,3,1,0:T(8,128)(2,1)}, u32[]{:S(2)}) copy-start(bf16[4,4,128,8,64]{2,4,3,1,0:T(8,128)(2,1)} %copy.39) | copy-start | bytes 6291460
  332.1 5.1 %copy-start.7 = (bf16[4,4,128,8,64]{2,4,3,1,0:T(8,128)(2,1)S(1)}, bf16[4,4,128,8,64]{2,4,3,1,0:T(8,128)(2,1)}, u32[]{:S(2)}) copy-start(bf16[4,4,128,8,64]{2,4,3,1,0:T(8,128)(2,1)} %get-tuple-element.226) | copy-start | bytes 6291460 | tf_op jit(solution)/shard_map/while
  334.9 5.2 %copy-start.2 = (f32[4,8,128,384]{3,2,1,0:T(8,128)}, f32[4,8,128,384]{3,2,1,0:T(8,128)S(1)}, u32[]{:S(2)}) copy-start(f32[4,8,128,384]{3,2,1,0:T(8,128)S(1)} %get-tuple-element.198) | copy-start | bytes 18874372 | tf_op jit(solution)/shard_map/while
  349.7 5.1 %copy-start.7 = (bf16[4,4,128,8,64]{2,4,3,1,0:T(8,128)(2,1)S(1)}, bf16[4,4,128,8,64]{2,4,3,1,0:T(8,128)(2,1)}, u32[]{:S(2)}) copy-start(bf16[4,4,128,8,64]{2,4,3,1,0:T(8,128)(2,1)} %get-tuple-element.226) | copy-start | bytes 6291460 | tf_op jit(solution)/shard_map/while
  352.5 5.2 %copy-start.2 = (f32[4,8,128,384]{3,2,1,0:T(8,128)}, f32[4,8,128,384]{3,2,1,0:T(8,128)S(1)}, u32[]{:S(2)}) copy-start(f32[4,8,128,384]{3,2,1,0:T(8,128)S(1)} %get-tuple-element.198) | copy-start | bytes 18874372 | tf_op jit(solution)/shard_map/while
  367.4 5.1 %copy-start.7 = (bf16[4,4,128,8,64]{2,4,3,1,0:T(8,128)(2,1)S(1)}, bf16[4,4,128,8,64]{2,4,3,1,0:T(8,128)(2,1)}, u32[]{:S(2)}) copy-start(bf16[4,4,128,8,64]{2,4,3,1,0:T(8,128)(2,1)} %get-tuple-element.226) | copy-start | bytes 6291460 | tf_op jit(solution)/shard_map/while
  370.2 5.2 %copy-start.2 = (f32[4,8,128,384]{3,2,1,0:T(8,128)}, f32[4,8,128,384]{3,2,1,0:T(8,128)S(1)}, u32[]{:S(2)}) copy-start(f32[4,8,128,384]{3,2,1,0:T(8,128)S(1)} %get-tuple-element.198) | copy-start | bytes 18874372 | tf_op jit(solution)/shard_map/while
  385.1 5.1 %copy-start.7 = (bf16[4,4,128,8,64]{2,4,3,1,0:T(8,128)(2,1)S(1)}, bf16[4,4,128,8,64]{2,4,3,1,0:T(8,128)(2,1)}, u32[]{:S(2)}) copy-start(bf16[4,4,128,8,64]{2,4,3,1,0:T(8,128)(2,1)} %get-tuple-element.226) | copy-start | bytes 6291460 | tf_op jit(solution)/shard_map/while
  387.9 5.2 %copy-start.2 = (f32[4,8,128,384]{3,2,1,0:T(8,128)}, f32[4,8,128,384]{3,2,1,0:T(8,128)S(1)}, u32[]{:S(2)}) copy-start(f32[4,8,128,384]{3,2,1,0:T(8,128)S(1)} %get-tuple-element.198) | copy-start | bytes 18874372 | tf_op jit(solution)/shard_map/while
  402.7 99.0 %copy-start.4 = (bf16[4,4,384,8,64]{2,4,3,1,0:T(8,128)(2,1)S(1)}, bf16[4,4,384,8,64]{2,4,3,1,0:T(8,128)(2,1)}, u32[]{:S(2)}) copy-start(bf16[4,4,384,8,64]{2,4,3,1,0:T(8,128)(2,1)} %get-tuple-element.50) | copy-start | bytes 18874372
  402.7 99.0 %copy-start.5 = (bf16[4,4,384,8,64]{2,4,3,1,0:T(8,128)(2,1)S(1)}, bf16[4,4,384,8,64]{2,4,3,1,0:T(8,128)(2,1)}, u32[]{:S(2)}) copy-start(bf16[4,4,384,8,64]{2,4,3,1,0:T(8,128)(2,1)} %get-tuple-element.51) | copy-start | bytes 18874372
  406.7 95.0 %collective-permute-start.2 = (bf16[2,16,128,512]{2,3,1,0:T(8,128)(2,1)S(1)}, bf16[2,16,128,512]{2,3,1,0:T(8,128)(2,1)S(1)}, u32[]{:S(2)}, u32[]{:S(2)}) collective-permute-start(bf16[2,16,128,512]{2,3,1,0:T(8,128)(2,1)S(1)} %get-tuple-element.135), channel_id=1, source_target_pairs={{0,1},{1,2},{2,3},{3,4},{4,5},{5,6},{6,7},{7,8},{8,9},{9,10},{10,1... | collective-permute-start | bytes 12582920 | tf_op jit(solution)/shard_map/ppermute | solution.py:27
  409.3 92.4 %collective-permute-start.3 = (bf16[2,16,128,512]{2,3,1,0:T(8,128)(2,1)S(1)}, bf16[2,16,128,512]{2,3,1,0:T(8,128)(2,1)S(1)}, u32[]{:S(2)}, u32[]{:S(2)}) collective-permute-start(bf16[2,16,128,512]{2,3,1,0:T(8,128)(2,1)S(1)} %get-tuple-element.136), channel_id=1, source_target_pairs={{1,0},{2,1},{3,2},{4,3},{5,4},{6,5},{7,6},{8,7},{9,8},{10,9},{11,1... | collective-permute-start | bytes 12582920 | tf_op jit(solution)/shard_map/ppermute | solution.py:27
  503.7 8.2 %copy-start.1 = (bf16[1024,512]{1,0:T(8,128)(2,1)S(1)}, bf16[1024,512]{1,0:T(8,128)(2,1)}, u32[]{:S(2)}) copy-start(bf16[1024,512]{1,0:T(8,128)(2,1)} %param.19) | copy-start | bytes 3145732
where the time goes:
time: 513 us; the launch traced here: 512 us
  waiting for transfers between devices  156 us (30%)
  local copies, waits for them, and re-layouts  103 us (20%)
  blocking collectives  98.4 us (19%)
  matrix products  82.8 us (16%)
  other arithmetic  58.4 us (11%)
  starting transfers between devices  11.9 us (2%)
    all_to_all x1, blocking collectives, on_device(): lax.all_to_all(normed, 'bus', split_axis=1, concat_axis=0, tiled=True)  98.4 us
    ppermute x2, waiting for transfers between devices, from_behind(): lax.ppermute(value, axis, [(source, source + steps) for source in range(l...  88.9 us
    ppermute x1, waiting for transfers between devices, with_halo(): before = lax.ppermute(last, axis, up)  66.6 us
    unnamed x27, local copies, waits for them, and re-layouts  39.7 us
    convert_element_type x1, local copies, waits for them, and re-layouts, on_device(): normed = (mixed * lax.rsqrt(jnp.mean(mixed * mixed, axis=-1, keepdims=Tru...  28.7 us
    unnamed x1, other arithmetic  25.9 us
    dot_general x4, matrix products, reader_terms(): jnp.einsum('shij,sihd->sjhd', dscores, queries, preferred_element_type=jn...  24.6 us
    dot_general x3, matrix products, on_device(): jnp.dot(flat_rows, weight, preferred_element_type=jnp.float32)  21.8 us
  transfers between devices with their start and end apart: 4, of which 2 were waited for; matrix products, arithmetic and copies ran while one was open for 4% of the time, Pallas kernels for 0%

commit v1 on v0

--- a/solution.py
+++ b/solution.py
@@ -96,7 +96,10 @@
     normed = (
         mixed * lax.rsqrt(jnp.mean(mixed * mixed, axis=-1, keepdims=True) + EPSILON) * norm_gain
     ).astype(jnp.bfloat16)
-    arrived = lax.all_to_all(normed, "bus", split_axis=1, concat_axis=0, tiled=True)
+    arrived = jnp.concatenate(
+        lax.all_to_all(jnp.stack(jnp.split(normed, lax.axis_size("bus"), axis=1)), "bus", 0, 0),
+        axis=0,
+    )
     flat_rows = arrived.reshape(-1, arrived.shape[2])
     queries, key_rows, value_rows = [
         jnp.dot(flat_rows, weight, preferred_element_type=jnp.float32)

time: 513 us -> 432 us (0.84)
  local copies, waits for them, and re-layouts: 103 us -> 53.8 us
  other arithmetic: 58.4 us -> 32.4 us
  matrix products: 82.8 us -> 76.1 us
    convert_element_type x1 -> x0, local copies, waits for them, and re-layouts: 28.7 us -> none  [on_device(): normed = (mixed * lax.rsqrt(jnp.mean(mixed * mixed, axis=-1, keepdims=Tru...]
    unnamed x1 -> x2, other arithmetic: 25.9 us -> 0.01 us
    unnamed x27 -> x47, local copies, waits for them, and re-layouts: 39.7 us -> 15.9 us
    dot_general x3, matrix products: 21.8 us -> 15.7 us  [on_device(): jnp.dot(flat_rows, weight, preferred_element_type=jnp.float32)]
  transfers between devices with their start and end apart: 4 -> 4, of which waited for: 2 -> 2; matrix products, arithmetic and copies ran while one was open for 4% -> 5% of each run, Pallas kernels for 0% -> 0%
where the time goes in v1:
time: 432 us; the launch traced here: 431 us
  waiting for transfers between devices  157 us (36%)
  blocking collectives  98.1 us (23%)
  matrix products  76.1 us (18%)
  local copies, waits for them, and re-layouts  53.8 us (12%)
  other arithmetic  32.4 us (8%)
  starting transfers between devices  11.9 us (3%)
    all_to_all x1, blocking collectives, on_device(): lax.all_to_all(jnp.stack(jnp.split(normed, lax.axis_size('bus'), axis=1))...  98.1 us
    ppermute x2, waiting for transfers between devices, from_behind(): lax.ppermute(value, axis, [(source, source + steps) for source in range(l...  89 us
    ppermute x1, waiting for transfers between devices, with_halo(): before = lax.ppermute(last, axis, up)  67.7 us
    dot_general x4, matrix products, reader_terms(): jnp.einsum('shij,sihd->sjhd', dscores, queries, preferred_element_type=jn...  24.7 us
    unnamed x47, local copies, waits for them, and re-layouts  15.9 us
    dot_general x3, matrix products, on_device(): jnp.dot(flat_rows, weight, preferred_element_type=jnp.float32)  15.7 us
    dot_general x4, matrix products, reader_terms(): jnp.einsum('shij,sjhd->sihd', weights_b, value_tiles, preferred_element_t...  13.8 us
    gather x1, local copies, waits for them, and re-layouts, on_device(): ordered = jnp.take(series, bus_order, axis=1)  13.7 us
  transfers between devices with their start and end apart: 4, of which 2 were waited for; matrix products, arithmetic and copies ran while one was open for 5% of the time, Pallas kernels for 0%

profile of v1, /device:TPU:12, one launch (start us, length us, event | category | flops | bytes accessed | tf_op | source)
XLA Modules:
  0.0 430.9 jit_solution(9947494288320202125)
XLA Ops:
  0.6 0.0 copy-start
  0.6 0.8 fusion.72
  1.4 0.7 compare_and_fusion
  2.8 0.0 copy-start.7
  2.8 13.7 %gather_fusion = bf16[2048,1024]{1,0:T(8,128)(2,1)} fusion(bf16[2048,1024]{1,0:T(8,128)(2,1)} %bitcast.180, s32[2048]{0:T(1024)S(1)} %fusion.72), kind=kCustom, calls=%fused_computation | custom fusion | bytes 8396800 | tf_op jit(solution)/shard_map/jit(_take)/gather | solution.py:90
  16.6 0.1 fusion.74
  16.7 3.6 multiply_reduce_fusion
  20.3 1.7 multiply_convert_fusion.6
  22.4 98.1 %all_to_all.5 = bf16[16,1,128,1024]{3,2,1,0:T(8,128)(2,1)S(1)} all-to-all(bf16[16,1,128,1024]{3,2,1,0:T(8,128)(2,1)S(1)} %fusion.56), channel_id=1, replica_groups=mesh['grp'=2,'bus'=16] {'bus'}, dimensions={0} | all-to-all | bytes 8388608 | tf_op jit(solution)/shard_map/all_to_all | solution.py:100
  120.6 3.7 convolution_convert_fusion.2
  124.3 3.1 copy.19
  127.5 5.9 %convolution_convert_fusion.1 = bf16[2048,512]{1,0:T(8,128)(2,1)} fusion(bf16[2048,1024]{1,0:T(8,128)(2,1)} %bitcast.192, bf16[1024,512]{1,0:T(8,128)(2,1)S(1)} %copy-done.10), kind=kOutput, calls=%fused_computation.57 | convolution fusion | flops 2148532224 | bytes 7340032 | tf_op jit(solution)/shard_map/dot_general | solution.py:105
  133.3 3.9 copy.20
  137.2 3.9 pad_maximum_fusion.2
  141.1 2.3 collective-permute-start
  143.5 3.5 collective-permute-start.1
  147.0 3.9 copy.21
  151.0 0.2 fusion.73
  151.2 6.1 %convolution_convert_fusion.3 = bf16[2048,512]{1,0:T(8,128)(2,1)} fusion(bf16[2048,1024]{1,0:T(8,128)(2,1)} %bitcast.193, bf16[1024,512]{1,0:T(8,128)(2,1)} %param.18), kind=kOutput, calls=%fused_computation.59 | convolution fusion | flops 2148532224 | bytes 7340032 | tf_op jit(solution)/shard_map/dot_general | solution.py:105
  157.3 6.2 %reshape.213 = bf16[4,4,128,8,64]{4,3,2,1,0:T(8,128)(2,1)} reshape(bf16[2048,512]{1,0:T(8,128)(2,1)} %convolution_convert_fusion.3) | data formatting | bytes 4194304 | tf_op jit(solution)/shard_map/reshape;reshape;reshape | solution.py:37
  163.6 5.1 %copy.22 = bf16[4,4,128,8,64]{2,4,3,1,0:T(8,128)(2,1)} copy(bf16[4,4,128,8,64]{4,3,2,1,0:T(8,128)(2,1)} %reshape.213) | data formatting | bytes 4194304
  168.6 67.7 %collective-permute-done = bf16[2,16,128,512]{2,3,1,0:T(8,128)(2,1)} collective-permute-done((bf16[2,16,128,512]{2,3,1,0:T(8,128)(2,1)}, bf16[2,16,128,512]{2,3,1,0:T(8,128)(2,1)}, u32[]{:S(2)}, u32[]{:S(2)}) %collective-permute-start) | collective-permute-done | bytes 4194336 | tf_op jit(solution)/shard_map/ppermute | solution.py:18
  236.3 0.0 collective-permute-done.1
  236.4 6.3 %pad_maximum_fusion = bf16[2,16,384,512]{2,3,1,0:T(8,128)(2,1)S(1)} fusion(bf16[2,16,128,512]{2,3,1,0:T(8,128)(2,1)} %collective-permute-done.1, bf16[1,16,128,512]{2,3,1,0:T(8,128)(2,1)} %copy.20, bf16[1,16,128,512]{2,3,1,0:T(8,128)(2,1)S(1)} %copy.19, bf16[2,16,128,512]{2,3,1,0:T(8,128)(2,1)} %collective-permute-done), kind=kLoop, calls=%fused_computation.47 | loop fusion | flops 50331648 | bytes 25165824 | tf_op jit(solution)/shard_map/concatenate | solution.py:20
  242.7 0.0 copy-start.4
  242.7 5.8 %fusion.79 = (bf16[1,16,384,512]{2,3,1,0:T(8,128)(2,1)}, bf16[1,16,384,512]{2,3,1,0:T(8,128)(2,1)}) fusion(bf16[2,16,384,512]{2,3,1,0:T(8,128)(2,1)S(1)} %pad_maximum_fusion), kind=kLoop, calls=%fused_computation.106 | loop fusion | bytes 25165824 | tf_op jit(solution)/shard_map/slice | solution.py:119
  248.5 73.1 %while.13 = (s32[]{:T(128)}, bf16[4,4,384,8,64]{2,4,3,1,0:T(8,128)(2,1)}, bf16[4,4,384,8,64]{2,4,3,1,0:T(8,128)(2,1)}, bf16[4,4,128,8,64]{2,4,3,1,0:T(8,128)(2,1...) while((s32[]{:T(128)}, ...), condition=%wide.region_4.5_spmd.clone, body=%wide.region_1.0_spmd.clone.sunk | while | flops 1044111360 | bytes 75687264 | solution.py:41
  248.5 0.1 broadcast_bitcast_fusion.2
  248.5 2.6 fusion.103
  251.2 2.3 exponential_reduce_fusion.2
  253.5 0.8 copy-done.6
  254.3 2.8 bitcast_dynamic-update-slice_fusion.5
  257.1 3.4 fusion.104
  260.6 6.2 %bitcast_dynamic-update-slice_fusion.4 = bf16[4,4,384,8,64]{2,4,3,1,0:T(8,128)(2,1)} fusion(bf16[4,4,384,8,64]{2,4,3,1,0:T(8,128)(2,1)} %get-tuple-element.189, s32[]{:T(128)} %get-tuple-element.188, f32[4,8,128,384]{3,2,1,0:T(8,128)} %copy-done.2, f32[4,8,128]{2,1,0:T(8,128)S(1)} %fusion.104, f32[4,8,128]{2,1,0:T(8,128)S(1)} %log_add_fusion.2, ...), kind=kOutput, calls=%fused_computation.17.clone.1 | convolution fusion | flops 414449664 | bytes 10521600 | tf_op jit(solution)/shard_map/while/body/eval_jaxpr/shij,sihd->sjhd/dot_general | solution.py:68
  266.7 0.1 broadcast_bitcast_fusion.2
  266.8 2.6 fusion.103
  269.4 2.3 exponential_reduce_fusion.2
  271.8 0.8 copy-done.6
  272.6 2.8 bitcast_dynamic-update-slice_fusion.5
  275.4 3.4 fusion.104
  278.8 6.2 %bitcast_dynamic-update-slice_fusion.4 = bf16[4,4,384,8,64]{2,4,3,1,0:T(8,128)(2,1)} fusion(bf16[4,4,384,8,64]{2,4,3,1,0:T(8,128)(2,1)} %get-tuple-element.189, s32[]{:T(128)} %get-tuple-element.188, f32[4,8,128,384]{3,2,1,0:T(8,128)} %copy-done.2, f32[4,8,128]{2,1,0:T(8,128)S(1)} %fusion.104, f32[4,8,128]{2,1,0:T(8,128)S(1)} %log_add_fusion.2, ...), kind=kOutput, calls=%fused_computation.17.clone.1 | convolution fusion | flops 414449664 | bytes 10521600 | tf_op jit(solution)/shard_map/while/body/eval_jaxpr/shij,sihd->sjhd/dot_general | solution.py:68
  285.0 0.1 broadcast_bitcast_fusion.2
  285.1 2.6 fusion.103
  287.7 2.3 exponential_reduce_fusion.2
  290.1 0.8 copy-done.6
  290.8 2.8 bitcast_dynamic-update-slice_fusion.5
  293.7 3.4 fusion.104
  297.1 6.2 %bitcast_dynamic-update-slice_fusion.4 = bf16[4,4,384,8,64]{2,4,3,1,0:T(8,128)(2,1)} fusion(bf16[4,4,384,8,64]{2,4,3,1,0:T(8,128)(2,1)} %get-tuple-element.189, s32[]{:T(128)} %get-tuple-element.188, f32[4,8,128,384]{3,2,1,0:T(8,128)} %copy-done.2, f32[4,8,128]{2,1,0:T(8,128)S(1)} %fusion.104, f32[4,8,128]{2,1,0:T(8,128)S(1)} %log_add_fusion.2, ...), kind=kOutput, calls=%fused_computation.17.clone.1 | convolution fusion | flops 414449664 | bytes 10521600 | tf_op jit(solution)/shard_map/while/body/eval_jaxpr/shij,sihd->sjhd/dot_general | solution.py:68
  303.3 0.1 broadcast_bitcast_fusion.2
  303.3 2.6 fusion.103
  306.0 2.3 exponential_reduce_fusion.2
  308.3 0.8 copy-done.6
  309.1 2.8 bitcast_dynamic-update-slice_fusion.5
  311.9 3.4 fusion.104
  315.4 6.2 %bitcast_dynamic-update-slice_fusion.4 = bf16[4,4,384,8,64]{2,4,3,1,0:T(8,128)(2,1)} fusion(bf16[4,4,384,8,64]{2,4,3,1,0:T(8,128)(2,1)} %get-tuple-element.189, s32[]{:T(128)} %get-tuple-element.188, f32[4,8,128,384]{3,2,1,0:T(8,128)} %copy-done.2, f32[4,8,128]{2,1,0:T(8,128)S(1)} %fusion.104, f32[4,8,128]{2,1,0:T(8,128)S(1)} %log_add_fusion.2, ...), kind=kOutput, calls=%fused_computation.17.clone.1 | convolution fusion | flops 414449664 | bytes 10521600 | tf_op jit(solution)/shard_map/while/body/eval_jaxpr/shij,sihd->sjhd/dot_general | solution.py:68
  321.6 0.0 slice-start.3
  321.6 4.0 fusion.54
  325.6 2.3 collective-permute-start.2
  328.0 3.7 collective-permute-start.3
  331.7 89.0 %collective-permute-done.2 = bf16[2,16,128,512]{2,3,1,0:T(8,128)(2,1)S(1)} collective-permute-done((bf16[2,16,128,512]{2,3,1,0:T(8,128)(2,1)S(1)}, bf16[2,16,128,512]{2,3,1,0:T(8,128)(2,1)S(1)}, u32[]{:S(2)}, u32[]{:S(2)}) %collective-permute-start.2) | collective-permute-done | bytes 4194336 | tf_op jit(solution)/shard_map/ppermute | solution.py:27
  420.7 1.9 add_convert_fusion
  422.6 1.7 slice_bitcast_fusion
  424.3 4.0 copy.24
  428.3 2.6 copy.25
  (63 shorter events, 0.4 us)
Async XLA Ops:
  0.6 120.0 %copy-start = (bf16[1024,512]{1,0:T(8,128)(2,1)S(1)}, bf16[1024,512]{1,0:T(8,128)(2,1)}, u32[]{:S(2)}) copy-start(bf16[1024,512]{1,0:T(8,128)(2,1)} %param.19) | copy-start | bytes 3145732
  2.8 13.8 %copy-start.7 = (bf16[24,1024]{1,0:T(8,128)(2,1)S(1)}, bf16[24,1024]{1,0:T(8,128)(2,1)}, u32[]{:S(2)}) copy-start(bf16[24,1024]{1,0:T(8,128)(2,1)} %param.15) | copy-start | bytes 147460
  16.5 3.7 copy-start.3
  16.5 3.7 copy-start.8
  120.6 3.7 copy-start.5
  124.3 3.1 copy-start.10
  141.1 9.8 %copy-start.9 = (s32[16,3]{0,1:T(4,128)S(1)}, s32[16,3]{0,1:T(4,128)}, u32[]{:S(2)}) copy-start(s32[16,3]{0,1:T(4,128)} %param.22) | copy-start | bytes 580
  141.1 10.0 %copy-start.11 = (f32[8]{0:T(128)S(1)}, f32[8]{0:T(128)}, u32[]{:S(2)}) copy-start(f32[8]{0:T(128)} %param.21) | copy-start | bytes 100
  141.1 95.2 %collective-permute-start = (bf16[2,16,128,512]{2,3,1,0:T(8,128)(2,1)}, bf16[2,16,128,512]{2,3,1,0:T(8,128)(2,1)}, u32[]{:S(2)}, u32[]{:S(2)}) collective-permute-start(bf16[2,16,128,512]{2,3,1,0:T(8,128)(2,1)} %pad_maximum_fusion.2), channel_id=1, source_target_pairs={{0,1},{1,2},{2,3},{3,4},{4,5},{5,6},{6,7},{7,8},{8,9},{9,10},{10,1... | collective-permute-start | bytes 12582920 | tf_op jit(solution)/shard_map/ppermute | solution.py:18
  143.5 92.9 %collective-permute-start.1 = (bf16[2,16,128,512]{2,3,1,0:T(8,128)(2,1)}, bf16[2,16,128,512]{2,3,1,0:T(8,128)(2,1)}, u32[]{:S(2)}, u32[]{:S(2)}) collective-permute-start(bf16[2,16,128,512]{2,3,1,0:T(8,128)(2,1)} %pad_maximum_fusion.2), channel_id=1, source_target_pairs={{1,0},{2,1},{3,2},{4,3},{5,4},{6,5},{7,6},{8,7},{9,8},{10,9},{11,1... | collective-permute-start | bytes 12582920 | tf_op jit(solution)/shard_map/ppermute | solution.py:19
  242.7 5.8 %copy-start.4 = (bf16[4,4,128,8,64]{2,4,3,1,0:T(8,128)(2,1)S(1)}, bf16[4,4,128,8,64]{2,4,3,1,0:T(8,128)(2,1)}, u32[]{:S(2)}) copy-start(bf16[4,4,128,8,64]{2,4,3,1,0:T(8,128)(2,1)} %copy.22) | copy-start | bytes 6291460
  251.2 5.9 %copy-start.2 = (f32[4,8,128,384]{3,2,1,0:T(8,128)}, f32[4,8,128,384]{3,2,1,0:T(8,128)S(1)}, u32[]{:S(2)}) copy-start(f32[4,8,128,384]{3,2,1,0:T(8,128)S(1)} %get-tuple-element.176) | copy-start | bytes 18874372 | tf_op jit(solution)/shard_map/while
  251.2 3.1 copy-start.6
  269.4 5.9 %copy-start.2 = (f32[4,8,128,384]{3,2,1,0:T(8,128)}, f32[4,8,128,384]{3,2,1,0:T(8,128)S(1)}, u32[]{:S(2)}) copy-start(f32[4,8,128,384]{3,2,1,0:T(8,128)S(1)} %get-tuple-element.176) | copy-start | bytes 18874372 | tf_op jit(solution)/shard_map/while
  269.4 3.1 copy-start.6
  287.7 6.0 %copy-start.2 = (f32[4,8,128,384]{3,2,1,0:T(8,128)}, f32[4,8,128,384]{3,2,1,0:T(8,128)S(1)}, u32[]{:S(2)}) copy-start(f32[4,8,128,384]{3,2,1,0:T(8,128)S(1)} %get-tuple-element.176) | copy-start | bytes 18874372 | tf_op jit(solution)/shard_map/while
  287.7 3.1 copy-start.6
  306.0 6.0 %copy-start.2 = (f32[4,8,128,384]{3,2,1,0:T(8,128)}, f32[4,8,128,384]{3,2,1,0:T(8,128)S(1)}, u32[]{:S(2)}) copy-start(f32[4,8,128,384]{3,2,1,0:T(8,128)S(1)} %get-tuple-element.176) | copy-start | bytes 18874372 | tf_op jit(solution)/shard_map/while
  306.0 3.1 copy-start.6
  321.6 99.1 %slice-start = ((s8[6291456]{0:T(1024)(128)(4,1)}), s8[4194304]{0:T(1024)(128)(4,1)S(1)}, s32[]{:S(2)}) async-start(s8[6291456]{0:T(1024)(128)(4,1)} %bitcast.183), calls=%async_computation.1 | async-start | bytes 8388608
  321.6 99.1 %slice-start.2 = ((s8[6291456]{0:T(1024)(128)(4,1)}), s8[4194304]{0:T(1024)(128)(4,1)S(1)}, s32[]{:S(2)}) async-start(s8[6291456]{0:T(1024)(128)(4,1)} %bitcast.187), calls=%async_computation.3 | async-start | bytes 8388608
  321.6 99.1 %slice-start.1 = ((s8[6291456]{0:T(1024)(128)(4,1)}), s8[2097152]{0:T(1024)(128)(4,1)S(1)}, s32[]{:S(2)}) async-start(s8[6291456]{0:T(1024)(128)(4,1)} %bitcast.183), calls=%async_computation.2 | async-start | bytes 4194304
  321.6 99.1 %slice-start.3 = ((s8[6291456]{0:T(1024)(128)(4,1)}), s8[2097152]{0:T(1024)(128)(4,1)S(1)}, s32[]{:S(2)}) async-start(s8[6291456]{0:T(1024)(128)(4,1)} %bitcast.187), calls=%async_computation.4 | async-start | bytes 4194304
  325.6 95.0 %collective-permute-start.2 = (bf16[2,16,128,512]{2,3,1,0:T(8,128)(2,1)S(1)}, bf16[2,16,128,512]{2,3,1,0:T(8,128)(2,1)S(1)}, u32[]{:S(2)}, u32[]{:S(2)}) collective-permute-start(bf16[2,16,128,512]{2,3,1,0:T(8,128)(2,1)S(1)} %get-tuple-element.113), channel_id=1, source_target_pairs={{0,1},{1,2},{2,3},{3,4},{4,5},{5,6},{6,7},{7,8},{8,9},{9,10},{10,1... | collective-permute-start | bytes 12582920 | tf_op jit(solution)/shard_map/ppermute | solution.py:27
  328.0 92.7 %collective-permute-start.3 = (bf16[2,16,128,512]{2,3,1,0:T(8,128)(2,1)S(1)}, bf16[2,16,128,512]{2,3,1,0:T(8,128)(2,1)S(1)}, u32[]{:S(2)}, u32[]{:S(2)}) collective-permute-start(bf16[2,16,128,512]{2,3,1,0:T(8,128)(2,1)S(1)} %get-tuple-element.114), channel_id=1, source_target_pairs={{1,0},{2,1},{3,2},{4,3},{5,4},{6,5},{7,6},{8,7},{9,8},{10,9},{11,1... | collective-permute-start | bytes 12582920 | tf_op jit(solution)/shard_map/ppermute | solution.py:27
  424.3 6.6 %copy-start.1 = (bf16[1024,512]{1,0:T(8,128)(2,1)S(1)}, bf16[1024,512]{1,0:T(8,128)(2,1)}, u32[]{:S(2)}) copy-start(bf16[1024,512]{1,0:T(8,128)(2,1)} %param.19) | copy-start | bytes 3145732
